TPU v7x, 256 devices: a whole 4x4x8 slice. The times are simulated.
256 devices in a mesh: row: 8 (over y, core), col: 32 (over x, z).
Axes of the slice: x: 4, y: 4, z: 8, core: 2. Of those that a mesh axis runs over, the one named last changes fastest.
Arguments:
- columns: float32 [2048, 131072], P(None, ('row', 'col')), may hold values from -6000 to 6000
- seating: int32 [32], replicated, may hold values from 0 to 31, each once
Outputs:
- rotated: float32 [2048, 131072], P(None, ('row', 'col'))
All inputs are finite; a program needn't handle non-finite values.
Results may differ from a plain program's by a relative error of at most 0.0001.
Values sent between devices are 32-bit elements; how exact they have to be, the bound alone decides.
No kernel may reach another device: no remote copies, remote signals or barrier semaphores. Data moves between devices by JAX's collectives and lax.ppermute only.
A program may use at most 128 MiB of HBM per device.

v0:
```python
import jax
import jax.numpy as jnp
from jax import lax
from jax.sharding import PartitionSpec as P

BLOCK = 64
NS_STEPS = 5
highest = lax.Precision.HIGHEST


def rotation(pair_gram, total_rows):
    pair_width = pair_gram.shape[-1]
    frobenius = jnp.sqrt(jnp.sum(pair_gram * pair_gram, axis=(-2, -1), keepdims=True))
    current = pair_gram / frobenius
    identity = jnp.eye(pair_width, dtype=jnp.float32)
    inverse_root = jnp.broadcast_to(identity, pair_gram.shape)
    for newton_turn in range(NS_STEPS):
        factor = 1.5 * identity - 0.5 * jnp.matmul(inverse_root, current, precision=highest)
        current = jnp.matmul(current, factor, precision=highest)
        inverse_root = jnp.matmul(factor, inverse_root, precision=highest)
    return inverse_root * jnp.sqrt(total_rows / frobenius)


def pair_up(blocks, stride):
    count = blocks.shape[0]
    shaped = blocks.reshape(count // (2 * stride), 2, stride, blocks.shape[1], blocks.shape[2])
    return jnp.concatenate([shaped[:, 0], shaped[:, 1]], axis=2)


def split_pairs(rotated_pairs, stride):
    groups = rotated_pairs.shape[0]
    half_width = rotated_pairs.shape[2] // 2
    shaped = rotated_pairs.reshape(groups, stride, 2, half_width, rotated_pairs.shape[3])
    return jnp.transpose(shaped, (0, 2, 1, 3, 4)).reshape(
        groups * 2 * stride, half_width, rotated_pairs.shape[3]
    )


def body(columns, seating):
    block_count = seating.shape[0]
    rows_here = columns.shape[1]
    col_count = lax.axis_size("col")
    total_rows = float(rows_here * lax.axis_size("row") * col_count)
    seat_count = block_count // col_count
    seated = columns.reshape(block_count, BLOCK, rows_here)[seating].reshape(
        block_count * BLOCK, rows_here
    )
    current = seated.reshape(block_count, BLOCK, rows_here)
    for stride in (seat_count, block_count // 2):
        paired = pair_up(current, stride)
        partial_gram = jnp.einsum("gsam,gsbm->gsab", paired, paired, precision=highest)
        pair_gram = lax.psum(partial_gram, ("row", "col"))
        rotate = rotation(pair_gram, total_rows)
        moved = jnp.einsum("gsab,gsam->gsbm", rotate, paired, precision=highest)
        current = split_pairs(moved, stride)
    seated = current.reshape(block_count * BLOCK, rows_here)
    ordered = seated.reshape(block_count, BLOCK, rows_here)
    restored = jnp.zeros_like(ordered).at[seating].set(ordered)
    return restored.reshape(block_count * BLOCK, rows_here)


def solution(mesh):
    in_specs = (P(None, ("row", "col")), P())
    out_specs = P(None, ("row", "col"))
    return jax.shard_map(body, mesh=mesh, in_specs=in_specs, out_specs=out_specs, check_vma=False)
```

profile of v0, /device:TPU:2, one launch (start us, length us, event | category | flops | bytes accessed | tf_op | source)
XLA Modules:
  0.0 617.4 jit_solution(11122427788383581620)
XLA Ops:
  7.2 5.0 gather_fusion
  12.2 2.7 slice_bitcast_fusion.3
  15.0 1.3 copy-done
  16.3 5.0 fusion.4
  21.6 261.7 %all-reduce.3.cloned.1.call-done = f32[16,1,128,128]{3,2,0,1:T(8,128)} async-done(((f32[16,1,128,128]{3,2,0,1:T(8,128)}), f32[16,1,128,128]{3,2,0,1:T(8,128)}) %all-reduce.3.cloned.1.call-update) | async-done | bytes 1048592 | tf_op jit(solution)/shard_map/psum | solution.py:52
  283.3 1.5 multiply_reduce_fusion.1
  284.9 2.3 fusion.15
  288.2 1.3 fusion.19
  289.5 1.2 fusion.14
  290.7 1.2 fusion.35
  293.1 1.2 fusion.13
  295.5 1.2 fusion.36
  296.7 1.4 fusion.12
  300.6 1.2 fusion.11
  301.8 1.9 convolution_multiply_fusion.6
  303.7 3.8 fusion.2
  308.0 1.3 copy-done.2
  309.3 5.5 fusion.5
  314.8 257.9 %all-reduce.5.cloned.1.call-done = f32[1,16,128,128]{3,2,1,0:T(8,128)} async-done(((f32[1,16,128,128]{3,2,1,0:T(8,128)}), f32[1,16,128,128]{3,2,1,0:T(8,128)}) %all-reduce.5.cloned.1.call-update) | async-done | bytes 1048592 | tf_op jit(solution)/shard_map/psum | solution.py:52
  572.8 1.5 multiply_reduce_fusion
  574.3 2.3 fusion.10
  577.7 1.3 fusion.16
  579.0 1.2 fusion.9
  582.6 1.2 fusion.8
  585.0 1.4 fusion.42
  586.3 1.2 fusion.7
  590.0 1.2 fusion.6
  591.2 1.9 convolution_multiply_fusion
  593.1 3.8 fusion
  596.9 2.6 copy.5
  599.5 2.5 broadcast_in_dim.4
  602.1 8.3 %scatter_fusion = f32[32,64,512]{2,1,0:T(8,128)} fusion(f32[32,64,512]{2,1,0:T(8,128)} %broadcast_in_dim.4, s32[32]{0:T(128)S(1)} %compare_select_fusion, f32[32,64,512]{2,1,0:T(8,128)} %bitcast.98), kind=kCustom, calls=%fused_computation.1 | custom fusion | bytes 12583040 | tf_op jit(solution)/shard_map/scatter | solution.py:58
  (32 shorter events, 14.2 us)
Async XLA Ops:
  6.5 276.8 %all-reduce.3.cloned.1.call-start = ((), (), s32[]{:S(2)}) async-start(), calls=%async_computation | async-start | bytes 2097152 | tf_op jit(solution)/shard_map/psum | solution.py:52
  15.0 1.3 copy-start
  21.3 551.4 %all-reduce.5.cloned.1.call-start = ((), (), s32[]{:S(2)}) async-start(), calls=%async_computation.1 | async-start | bytes 2097152 | tf_op jit(solution)/shard_map/psum | solution.py:52
  283.3 4.9 copy-start.4
  299.4 4.3 copy-start.1
  308.0 1.3 copy-start.2
  572.8 4.9 copy-start.5
  588.8 4.3 copy-start.3
Sparse Core Ops, SparseCore 0:
  21.4 261.8 all-reduce.2
  315.0 257.7 all-reduce.4
where the time goes:
time: 622 us; the launch traced here: 617 us
  waiting for transfers between devices  520 us (84%)
  matrix products  55.4 us (9%)
  local copies, waits for them, and re-layouts  24.4 us (4%)
  between operations  13.9 us (2%)
    psum x2, waiting for transfers between devices, body(): pair_gram = lax.psum(partial_gram, ('row', 'col'))  520 us
    dot_general x10, matrix products, rotation(): jnp.matmul(inverse_root, current, precision=highest)  14.6 us
    dot_general x10, matrix products, rotation(): inverse_root = jnp.matmul(factor, inverse_root, precision=highest)  13.1 us
  transfers between devices with their start and end apart: 2, of which 2 were waited for; matrix products, arithmetic and copies ran while one was open for 0% of the time, Pallas kernels for 0%

commit v1 on v0

--- a/solution.py
+++ b/solution.py
@@ -49,7 +49,8 @@
     for stride in (seat_count, block_count // 2):
         paired = pair_up(current, stride)
         partial_gram = jnp.einsum("gsam,gsbm->gsab", paired, paired, precision=highest)
-        pair_gram = lax.psum(partial_gram, ("row", "col"))
+        one_axis = lax.psum(partial_gram, "col")
+        pair_gram = lax.psum(one_axis, "row")
         rotate = rotation(pair_gram, total_rows)
         moved = jnp.einsum("gsab,gsam->gsbm", rotate, paired, precision=highest)
         current = split_pairs(moved, stride)

time: 622 us -> 540 us (0.87)
  waiting for transfers between devices: 520 us -> 438 us
    psum x2 -> x4, waiting for transfers between devices: 520 us -> 438 us  [the longest x2 301 us: body(): one_axis = lax.psum(partial_gram, 'col')]
  transfers between devices with their start and end apart: 2 -> 4, of which waited for: 2 -> 4; matrix products, arithmetic and copies ran while one was open for 0% -> 0% of each run, Pallas kernels for 0% -> 0%
where the time goes in v1:
time: 540 us; the launch traced here: 535 us
  waiting for transfers between devices  438 us (81%)
  matrix products  55.3 us (10%)
  local copies, waits for them, and re-layouts  24.4 us (5%)
  between operations  13.7 us (3%)
    psum x2, waiting for transfers between devices, body(): one_axis = lax.psum(partial_gram, 'col')  301 us
    psum x2, waiting for transfers between devices, body(): pair_gram = lax.psum(one_axis, 'row')  137 us
    dot_general x10, matrix products, rotation(): jnp.matmul(inverse_root, current, precision=highest)  15 us
    dot_general x10, matrix products, rotation(): inverse_root = jnp.matmul(factor, inverse_root, precision=highest)  13 us
  transfers between devices with their start and end apart: 4, of which 4 were waited for; matrix products, arithmetic and copies ran while one was open for 0% of the time, Pallas kernels for 0%

profile of v1, /device:TPU:2, one launch (start us, length us, event | category | flops | bytes accessed | tf_op | source)
XLA Modules:
  0.0 535.2 jit_solution(15081239934047286879)
XLA Ops:
  7.2 5.0 gather_fusion
  12.2 2.7 slice_bitcast_fusion.3
  15.0 1.3 copy-done
  16.3 5.0 fusion.4
  21.4 152.1 %all-reduce.5.cloned.1.call-done = f32[16,1,128,128]{3,2,0,1:T(8,128)} async-done(((f32[16,1,128,128]{3,2,0,1:T(8,128)}), f32[16,1,128,128]{3,2,0,1:T(8,128)}) %all-reduce.5.cloned.1.call-update) | async-done | bytes 1048592 | tf_op jit(solution)/shard_map/psum | solution.py:52
  173.7 68.5 %all-reduce.7.cloned.1.call-done = f32[16,1,128,128]{3,2,0,1:T(8,128)} async-done(((f32[16,1,128,128]{3,2,0,1:T(8,128)}), f32[16,1,128,128]{3,2,0,1:T(8,128)}) %all-reduce.7.cloned.1.call-update) | async-done | bytes 1048592 | tf_op jit(solution)/shard_map/psum | solution.py:53
  242.2 1.5 multiply_reduce_fusion.1
  243.8 2.3 fusion.15
  247.2 1.3 fusion.19
  248.4 1.2 fusion.14
  252.0 1.2 fusion.13
  255.7 1.6 fusion.12
  259.7 1.2 fusion.11
  260.9 1.9 convolution_multiply_fusion.6
  262.8 3.8 fusion.2
  267.1 1.3 copy-done.2
  268.4 5.2 fusion.5
  273.7 148.4 %all-reduce.9.cloned.1.call-done = f32[1,16,128,128]{3,2,1,0:T(8,128)} async-done(((f32[1,16,128,128]{3,2,1,0:T(8,128)}), f32[1,16,128,128]{3,2,1,0:T(8,128)}) %all-reduce.9.cloned.1.call-update) | async-done | bytes 1048592 | tf_op jit(solution)/shard_map/psum | solution.py:52
  422.2 68.7 %all-reduce.11.cloned.1.call-done = f32[1,16,128,128]{3,2,1,0:T(8,128)} async-done(((f32[1,16,128,128]{3,2,1,0:T(8,128)}), f32[1,16,128,128]{3,2,1,0:T(8,128)}) %all-reduce.11.cloned.1.call-update) | async-done | bytes 1048592 | tf_op jit(solution)/shard_map/psum | solution.py:53
  490.9 1.5 multiply_reduce_fusion
  492.4 2.3 fusion.10
  495.8 1.3 fusion.16
  497.1 1.2 fusion.9
  500.7 1.2 fusion.8
  501.9 1.2 fusion.43
  504.3 1.4 fusion.7
  508.1 1.2 fusion.6
  509.3 1.9 convolution_multiply_fusion
  511.3 3.8 fusion
  515.0 2.6 copy.5
  517.7 2.5 broadcast_in_dim.4
  520.2 8.3 %scatter_fusion = f32[32,64,512]{2,1,0:T(8,128)} fusion(f32[32,64,512]{2,1,0:T(8,128)} %broadcast_in_dim.4, s32[32]{0:T(128)S(1)} %compare_select_fusion, f32[32,64,512]{2,1,0:T(8,128)} %bitcast.98), kind=kCustom, calls=%fused_computation.1 | custom fusion | bytes 12583040 | tf_op jit(solution)/shard_map/scatter | solution.py:59
  (38 shorter events, 16.7 us)
Async XLA Ops:
  6.5 166.9 %all-reduce.5.cloned.1.call-start = ((), (), s32[]{:S(2)}) async-start(), calls=%async_computation | async-start | bytes 2097152 | tf_op jit(solution)/shard_map/psum | solution.py:52
  15.0 1.3 copy-start
  21.3 220.9 %all-reduce.7.cloned.1.call-start = ((), (), s32[]{:S(2)}) async-start(), calls=%async_computation.1 | async-start | bytes 2097152 | tf_op jit(solution)/shard_map/psum | solution.py:53
  173.4 248.7 %all-reduce.9.cloned.1.call-start = ((), (), s32[]{:S(2)}) async-start(), calls=%async_computation.2 | async-start | bytes 2097152 | tf_op jit(solution)/shard_map/psum | solution.py:52
  242.2 4.9 copy-start.4
  258.5 4.3 copy-start.1
  267.1 1.3 copy-start.2
  273.7 217.2 %all-reduce.11.cloned.1.call-start = ((), (), s32[]{:S(2)}) async-start(), calls=%async_computation.3 | async-start | bytes 2097152 | tf_op jit(solution)/shard_map/psum | solution.py:53
  490.9 4.9 copy-start.5
  506.9 4.3 copy-start.3
Sparse Core Ops, SparseCore 0:
  21.4 151.9 all-reduce.4
  175.8 66.4 all-reduce.6
  273.8 148.3 all-reduce.8
  424.4 66.4 all-reduce.10
